TPU v7x, 32 devices: a whole 2x2x4 slice. The times are simulated.
32 devices in a mesh: grp: 2 (over y), seq: 16 (over z, x, core).
Axes of the slice: x: 2, y: 2, z: 4, core: 2. Of those that a mesh axis runs over, the one named last changes fastest.
Arguments:
- query: bfloat16 [2, 16, 1024, 128], P('grp', None, 'seq'), parts along dimension 0, may hold values from -49 to 49
- key: bfloat16 [2, 16, 1024, 128], P('grp', None, 'seq'), parts along dimension 0, may hold values from -8 to 8
- value: bfloat16 [2, 16, 1024, 128], P('grp', None, 'seq'), parts along dimension 0, may hold values from -6 to 6
- mem_key: bfloat16 [2, 16, 1024, 128], P('grp', None, 'seq'), parts along dimension 0, may hold values from -8 to 8
- mem_value: bfloat16 [2, 16, 1024, 128], P('grp', None, 'seq'), parts along dimension 0, may hold values from -6 to 6
- mem_count: int32 [2, 4], P('grp'), parts along dimension 0, may hold values from 1 to 256, as said below
- mem_factor: int32 [2, 4], P('grp'), parts along dimension 0, may hold values from 1 to 16, as said below
- out_weight: bfloat16 [2048, 3072], P('seq'), may hold values from -0.125 to 0.125
Outputs:
- block_out: bfloat16 [2, 1024, 3072], P('grp', 'seq'), parts along dimension 0
There are 2 independent parts, one for each index of `grp`. A program takes and returns all parts, laid end to end along the dimension named above; an argument that names none is the same for every part. Nothing has to cross between parts.
Inputs may be any that keep to these rules, and one draw needn't show every extreme that they name: `mem_count`: some stretch of every sequence holds exactly 256 live tokens. `mem_factor`: powers of two.
All inputs are finite; a program needn't handle non-finite values.
Results may differ from a plain program's by a relative error of at most 0.0052.
Values may be sent and summed in bfloat16 or wider, within the bound.
A program may use at most 128 MiB of HBM per device.

v0:
```python
import jax
import jax.numpy as jnp
from jax import lax
from jax.sharding import PartitionSpec as P

MCAP = 256


def per_device(query, key, value, mem_key, mem_value, mem_count, mem_factor, out_weight):
    seqs, heads, rows, width = query.shape
    slots_dev = mem_key.shape[2]
    devices = lax.axis_size("seq")
    groups = seqs * heads
    copies = devices // groups
    half = rows // copies
    feat = out_weight.shape[1]
    own_queries = (
        query.reshape(groups, half, copies, width)
        .transpose(0, 2, 1, 3)
        .reshape(groups * copies, half, width)
    )

    def spread(array, count):
        widened = jnp.broadcast_to(
            array.reshape(groups, 1, count, width), (groups, copies, count, width)
        )
        return widened.reshape(groups * copies, count, width)

    head_q, head_k, head_v, head_mk, head_mv = (
        lax.all_to_all(own_queries, "seq", split_axis=0, concat_axis=1, tiled=True),
        lax.all_to_all(spread(key, rows), "seq", split_axis=0, concat_axis=1, tiled=True),
        lax.all_to_all(spread(value, rows), "seq", split_axis=0, concat_axis=1, tiled=True),
        lax.all_to_all(spread(mem_key, slots_dev), "seq", split_axis=0, concat_axis=1, tiled=True),
        lax.all_to_all(
            spread(mem_value, slots_dev), "seq", split_axis=0, concat_axis=1, tiled=True
        ),
    )
    length_q = head_q.shape[1]
    length = head_k.shape[1]
    slots = head_mk.shape[1]
    seq_index = lax.axis_index("seq") // copies // heads
    counts = lax.dynamic_index_in_dim(mem_count, seq_index, 0, keepdims=False)
    factors = lax.dynamic_index_in_dim(mem_factor, seq_index, 0, keepdims=False)
    slot = jnp.arange(slots)
    stretch_of = slot // MCAP
    offset = slot % MCAP
    picked = stretch_of[:, None] == jnp.arange(counts.shape[0])[None, :]
    slot_count = jnp.sum(jnp.where(picked, counts[None, :], 0), 1)
    slot_factor = jnp.sum(jnp.where(picked, factors[None, :], 0), 1)
    bias = jnp.where(
        offset < slot_count, jnp.log(slot_factor.astype(jnp.float32)), jnp.float32(-1000000000.0)
    )
    full_bias = jnp.concatenate([jnp.zeros((length,), jnp.float32), bias])
    all_keys = jnp.concatenate([head_k[0], head_mk[0]], 0)
    all_vals = jnp.concatenate([head_v[0], head_mv[0]], 0)
    scale = width ** (-0.5)
    block = min(512, length_q)
    query_blocks = head_q[0].reshape(length_q // block, block, width)

    def attend(queries):
        score = (
            jnp.einsum("qd,kd->qk", queries, all_keys, preferred_element_type=jnp.float32) * scale
        )
        score = score + full_bias[None, :]
        top = jnp.max(score, axis=1, keepdims=True)
        prob = jnp.exp(score - top)
        total = jnp.sum(prob, axis=1, keepdims=True)
        weight = prob.astype(jnp.bfloat16)
        attended = jnp.dot(weight, all_vals, preferred_element_type=jnp.float32) / total
        return attended.astype(jnp.bfloat16)

    attended = lax.map(attend, query_blocks).reshape(1, length_q, width)
    returned = lax.all_to_all(attended, "seq", split_axis=1, concat_axis=0, tiled=True)
    columns = returned.reshape(seqs, heads, copies, half, width).transpose(0, 3, 2, 1, 4)
    columns = columns.reshape(seqs * rows, heads * width)
    mixed = jnp.dot(
        columns,
        lax.all_gather(out_weight, "seq", axis=0, tiled=True),
        preferred_element_type=jnp.float32,
    )
    result = mixed.reshape(seqs, rows, feat).astype(jnp.bfloat16)
    return result


def solution(mesh):
    in_specs = (
        P("grp", None, "seq", None),
        P("grp", None, "seq", None),
        P("grp", None, "seq", None),
        P("grp", None, "seq", None),
        P("grp", None, "seq", None),
        P("grp", None),
        P("grp", None),
        P("seq", None),
    )
    out_specs = P("grp", "seq", None)
    return jax.shard_map(
        per_device, mesh=mesh, in_specs=in_specs, out_specs=out_specs, check_vma=False
    )
```

profile of v0, /device:TPU:0, one launch (start us, length us, event | category | flops | bytes accessed | tf_op | source)
XLA Modules:
  0.0 152.8 jit_solution(13897523027870306095)
XLA Ops:
  6.5 0.0 all-gather.2.cloned.1.call-start
  6.5 0.7 all-gather.2.cloned.1.call-update
  7.3 17.4 %all_to_all.24 = bf16[16,64,128]{2,1,0:T(8,128)(2,1)S(1)} all-to-all(bf16[16,64,128]{2,1,0:T(8,128)(2,1)} %bitcast.58), channel_id=1, replica_groups=mesh['grp'=2,'seq'=16] {'seq'}, dimensions={0} | all-to-all | bytes 524288 | tf_op jit(solution)/shard_map/all_to_all | solution.py:31
  24.7 18.1 %all_to_all.25 = bf16[16,64,128]{2,1,0:T(8,128)(2,1)S(1)} all-to-all(bf16[16,64,128]{2,1,0:T(8,128)(2,1)} %bitcast.59), channel_id=1, replica_groups=mesh['grp'=2,'seq'=16] {'seq'}, dimensions={0} | all-to-all | bytes 524288 | tf_op jit(solution)/shard_map/all_to_all | solution.py:33
  42.8 17.7 %all_to_all.26 = bf16[16,64,128]{2,1,0:T(8,128)(2,1)S(1)} all-to-all(bf16[16,64,128]{2,1,0:T(8,128)(2,1)} %bitcast.60), channel_id=1, replica_groups=mesh['grp'=2,'seq'=16] {'seq'}, dimensions={0} | all-to-all | bytes 524288 | tf_op jit(solution)/shard_map/all_to_all | solution.py:32
  60.5 4.0 %all-to-all-start.4 = ((bf16[16,64,128]{2,1,0:T(8,128)(2,1)}), bf16[16,64,128]{2,1,0:T(8,128)(2,1)S(1)}, u32[]{:S(2)}, u32[]{:S(2)}) async-start(bf16[16,64,128]{2,1,0:T(8,128)(2,1)} %bitcast.61), calls=%async_computation.4 | async-start | bytes 524288 | tf_op jit(solution)/shard_map/all_to_all | solution.py:34
  64.5 0.8 select_reduce_fusion.1
  65.3 13.5 %all-to-all-done.4 = bf16[16,64,128]{2,1,0:T(8,128)(2,1)S(1)} async-done(((bf16[16,64,128]{2,1,0:T(8,128)(2,1)}), bf16[16,64,128]{2,1,0:T(8,128)(2,1)S(1)}, u32[]{:S(2)}, u32[]{:S(2)}) %all-to-all-start.4) | async-done | bytes 262176 | tf_op jit(solution)/shard_map/all_to_all | solution.py:34
  78.8 5.9 %all-to-all-start = ((bf16[16,64,128]{2,1,0:T(8,128)(2,1)}), bf16[16,64,128]{2,1,0:T(8,128)(2,1)S(1)}, u32[]{:S(2)}, u32[]{:S(2)}) async-start(bf16[16,64,128]{2,1,0:T(8,128)(2,1)} %bitcast.62), calls=%async_computation | async-start | bytes 524288 | tf_op jit(solution)/shard_map/all_to_all | solution.py:30
  84.8 14.5 %all-to-all-done = bf16[16,64,128]{2,1,0:T(8,128)(2,1)S(1)} async-done(((bf16[16,64,128]{2,1,0:T(8,128)(2,1)}), bf16[16,64,128]{2,1,0:T(8,128)(2,1)S(1)}, u32[]{:S(2)}, u32[]{:S(2)}) %all-to-all-start) | async-done | bytes 262176 | tf_op jit(solution)/shard_map/all_to_all | solution.py:30
  99.3 5.6 %while.10 = (s32[]{:T(128)}, bf16[2,512,128]{2,1,0:T(8,128)(2,1)S(1)}, bf16[2,512,128]{2,1,0:T(8,128)(2,1)S(1)}, bf16[2048,128]{1,0:T(8,128)(2,1)S(1)}, f32[2048...) while((s32[]{:T(128)}, bf16[2,512,128]{2,1,0:T(8,128)(2,1)S(1)}, ...), condition=%wide.region_5.6_spmd, body=%wide.region_2.5_spmd.sunk | while | flops 548535296 | bytes 13928533 | solution.py:72
  99.3 0.8 fusion.43
  100.1 1.0 fusion.44
  101.0 1.0 fusion.45
  102.1 0.8 fusion.43
  102.9 1.0 fusion.44
  103.8 1.0 fusion.45
  104.9 0.4 copy.22
  105.3 0.5 broadcast.60
  105.8 2.2 %reduce = bf16[1024,128]{1,0:T(8,128)(2,1)S(1)} reduce(bf16[1024,1,128]{2,1,0:T(2,128)(2,1)S(1)} %bitcast.50, bf16[]{:T(256)} %broadcast.60), dimensions={1}, to_apply=%bitcast.39.reduce_sub_computation | reduce | bytes 524290
  108.0 0.1 reshape.54
  108.1 20.1 %all_to_all.27 = bf16[16,2,4096]{2,1,0:T(2,128)(2,1)S(1)} all-to-all(bf16[16,2,4096]{2,1,0:T(2,128)(2,1)S(1)} %reshape.54), channel_id=1, replica_groups=mesh['grp'=2,'seq'=16] {'seq'}, dimensions={0} | all-to-all | bytes 524288 | tf_op jit(solution)/shard_map/all_to_all | solution.py:73
  128.2 0.3 reshape.55
  128.5 0.2 copy.14
  128.7 9.6 %all-gather.2.cloned.1.call-done = bf16[2048,3072]{1,0:T(8,128)(2,1)} async-done(((bf16[128,3072]{1,0:T(8,128)(2,1)}), bf16[2048,3072]{1,0:T(8,128)(2,1)}) %all-gather.2.cloned.1.call-update) | async-done | bytes 12582928 | tf_op jit(solution)/shard_map/all_gather | solution.py:78
  138.3 7.6 %fusion.22 = bf16[1,64,3072]{2,1,0:T(8,128)(2,1)} fusion(bf16[2048,3072]{1,0:T(8,128)(2,1)} %all-gather.2.cloned.1.call-done, bf16[8,8,16,128]{3,2,1,0:T(8,128)(2,1)S(1)} %bitcast.51), kind=kOutput, calls=%fused_computation.16 | convolution fusion | flops 805502976 | bytes 13238272 | tf_op jit(solution)/shard_map/dot_general | solution.py:76
  (7 shorter events, 0.1 us)
Async XLA Ops:
  6.5 131.8 %all-gather.2.cloned.1.call-start = ((), (), s32[]{:S(2)}) async-start(), calls=%async_computation.6 | async-start | bytes 13369344 | tf_op jit(solution)/shard_map/all_gather | solution.py:78
  60.5 18.3 %all-to-all-start.4 = ((bf16[16,64,128]{2,1,0:T(8,128)(2,1)}), bf16[16,64,128]{2,1,0:T(8,128)(2,1)S(1)}, u32[]{:S(2)}, u32[]{:S(2)}) async-start(bf16[16,64,128]{2,1,0:T(8,128)(2,1)} %bitcast.61), calls=%async_computation.4 | async-start | bytes 524288 | tf_op jit(solution)/shard_map/all_to_all | solution.py:34
  78.8 20.5 %all-to-all-start = ((bf16[16,64,128]{2,1,0:T(8,128)(2,1)}), bf16[16,64,128]{2,1,0:T(8,128)(2,1)S(1)}, u32[]{:S(2)}, u32[]{:S(2)}) async-start(bf16[16,64,128]{2,1,0:T(8,128)(2,1)} %bitcast.62), calls=%async_computation | async-start | bytes 524288 | tf_op jit(solution)/shard_map/all_to_all | solution.py:30
Sparse Core Ops, SparseCore 0:
  9.6 128.6 all-gather.1
where the time goes:
time: 154 us; the launch traced here: 153 us
  blocking collectives  73.4 us (48%)
  waiting for transfers between devices  38.3 us (25%)
  between operations  13.5 us (9%)
  matrix products  11.3 us (7%)
  starting transfers between devices  9.82 us (6%)
  other arithmetic  4.96 us (3%)
    all_to_all x1, blocking collectives, per_device(): lax.all_to_all(attended, 'seq', split_axis=1, concat_axis=0, tiled=True)  20.1 us
    all_to_all x1, blocking collectives, per_device(): lax.all_to_all(spread(mem_key, slots_dev), 'seq', split_axis=0, concat_ax...  18.1 us
    all_to_all x1, blocking collectives, per_device(): lax.all_to_all(spread(value, rows), 'seq', split_axis=0, concat_axis=1, t...  17.7 us
    all_to_all x1, blocking collectives, per_device(): lax.all_to_all(spread(key, rows), 'seq', split_axis=0, concat_axis=1, til...  17.4 us
    all_to_all x1, waiting for transfers between devices, per_device(): lax.all_to_all(own_queries, 'seq', split_axis=0, concat_axis=1, tiled=True)  14.5 us
    all_to_all x1, waiting for transfers between devices, per_device(): lax.all_to_all(spread(mem_value, slots_dev), 'seq', split_axis=0, concat_...  13.5 us
    all_gather x1, waiting for transfers between devices, per_device(): lax.all_gather(out_weight, 'seq', axis=0, tiled=True)  9.63 us
    dot_general x1, matrix products, per_device(): jnp.dot(columns, lax.all_gather(out_weight, 'seq', axis=0, tiled=True), p...  7.62 us
  transfers between devices with their start and end apart: 3, of which 3 were waited for; matrix products, arithmetic and copies ran while one was open for 7% of the time, Pallas kernels for 0%

commit v1 on v0

--- a/solution.py
+++ b/solution.py
@@ -1,6 +1,11 @@
+import functools
+import math
+
 import jax
 import jax.numpy as jnp
 from jax import lax
+from jax.experimental import pallas as pl
+from jax.experimental.pallas import tpu as pltpu
 from jax.sharding import PartitionSpec as P
 
 MCAP = 256
@@ -82,6 +87,146 @@
     return result
 
 
+def exchange_attend(n, scale2, q_hbm, k_hbm, v_hbm, mk_hbm, mv_hbm, bias_ref, out_ref,
+                    qbuf, kbuf, vbuf, att, in_send, in_recv, own_sem, ret_send, ret_recv):
+    me = lax.axis_index("seq")
+    rows, width = qbuf.shape[1], qbuf.shape[2]
+
+    barrier = pltpu.get_barrier_semaphore()
+
+    @pl.loop(1, n)
+    def _(step):
+        pl.semaphore_signal(barrier, inc=1, device_id={"seq": lax.rem(me + step, n)},
+                            device_id_type=pl.DeviceIdType.MESH)
+
+    pl.semaphore_wait(barrier, n - 1)
+
+    streams = (
+        (q_hbm, qbuf, 0), (k_hbm, kbuf, 0), (mk_hbm, kbuf, n), (v_hbm, vbuf, 0), (mv_hbm, vbuf, n),
+    )
+
+    def sending(a, peer):
+        src, dst, base = streams[a]
+        return pltpu.make_async_remote_copy(
+            src_ref=src.at[0, peer], dst_ref=dst.at[base + me],
+            send_sem=in_send.at[a, peer], recv_sem=in_recv.at[a, me],
+            device_id={"seq": peer}, device_id_type=pl.DeviceIdType.MESH)
+
+    def arriving(a, peer):
+        src, dst, base = streams[a]
+        return pltpu.make_async_remote_copy(
+            src_ref=src.at[0, peer], dst_ref=dst.at[base + peer],
+            send_sem=in_send.at[a, peer], recv_sem=in_recv.at[a, peer],
+            device_id={"seq": peer}, device_id_type=pl.DeviceIdType.MESH)
+
+    def own(a):
+        src, dst, base = streams[a]
+        return pltpu.make_async_copy(src.at[0, me], dst.at[base + me], own_sem.at[a])
+
+    for group in ((0, 1, 2), (3, 4)):
+        @pl.loop(0, n - 1)
+        def _(k):
+            peer = lax.rem(me + 1 + lax.rem(k + n // 2 - 1, n - 1), n)
+            for a in group:
+                sending(a, peer).start()
+    for a in range(5):
+        own(a).start()
+    for a in range(5):
+        own(a).wait()
+
+    @pl.loop(1, n)
+    def _(step):
+        peer = lax.rem(me + step, n)
+        for a in range(5):
+            arriving(a, peer).wait_recv()
+
+    keys = kbuf[...].reshape(2 * n * rows, width)
+    vals = vbuf[...].reshape(2 * n * rows, width)
+    parts = n // 4
+
+    def returning(owner):
+        return pltpu.make_async_remote_copy(
+            src_ref=att.at[owner],
+            dst_ref=out_ref.at[:, pl.ds(pl.multiple_of(me * width, width), width)],
+            send_sem=ret_send.at[owner], recv_sem=ret_recv.at[me],
+            device_id={"seq": owner}, device_id_type=pl.DeviceIdType.MESH)
+
+    @pl.loop(0, parts)
+    def _(j):
+        block = lax.rem(me // 4 + parts // 2 + j, parts)
+        queries = qbuf[pl.ds(block * 4, 4)].reshape(4 * rows, width)
+        score = lax.dot_general(queries, keys, (((1,), (1,)), ((), ())),
+                                preferred_element_type=jnp.float32)
+        score = score * scale2 + bias_ref[...]
+        top = jnp.max(score, axis=1, keepdims=True)
+        prob = jnp.exp2(score - top)
+        total = jnp.sum(prob, axis=1, keepdims=True)
+        mixed = jnp.dot(prob.astype(jnp.bfloat16), vals, preferred_element_type=jnp.float32)
+        att[pl.ds(block * 4, 4)] = (mixed / total).astype(jnp.bfloat16).reshape(4, rows, width)
+        for t in range(4):
+            owner = block * 4 + t
+
+            @pl.when(owner != me)
+            def _():
+                returning(owner).start()
+
+    mine = pltpu.make_async_copy(
+        att.at[me], out_ref.at[:, pl.ds(pl.multiple_of(me * width, width), width)], own_sem.at[0])
+    mine.start()
+    mine.wait()
+
+    @pl.loop(1, n)
+    def _(step):
+        peer = lax.rem(me + step, n)
+        for a in range(5):
+            sending(a, peer).wait_send()
+        returning(peer).wait_send()
+        pltpu.make_async_remote_copy(
+            src_ref=att.at[peer],
+            dst_ref=out_ref.at[:, pl.ds(pl.multiple_of(peer * width, width), width)],
+            send_sem=ret_send.at[peer], recv_sem=ret_recv.at[peer],
+            device_id={"seq": peer}, device_id_type=pl.DeviceIdType.MESH).wait_recv()
+
+
+def full_bias_of(counts, factors, length, slots):
+    slot = jnp.arange(slots)
+    picked = (slot // MCAP)[:, None] == jnp.arange(counts.shape[0])[None, :]
+    slot_count = jnp.sum(jnp.where(picked, counts[None, :], 0), 1)
+    slot_factor = jnp.sum(jnp.where(picked, factors[None, :], 0), 1)
+    bias = jnp.where(slot % MCAP < slot_count, jnp.log(slot_factor.astype(jnp.float32)),
+                     jnp.float32(-1000000000.0))
+    return jnp.concatenate([jnp.zeros((length,), jnp.float32), bias])[None, :]
+
+
+def per_device_direct(query, key, value, mem_key, mem_value, mem_count, mem_factor, out_weight):
+    _, heads, rows, width = query.shape
+    n = heads
+    log2e = math.log2(math.e)
+    bias = full_bias_of(mem_count[0], mem_factor[0], n * rows, n * rows) * log2e
+    weights = lax.all_gather(out_weight, "seq", axis=0, tiled=True)
+    columns = pl.pallas_call(
+        functools.partial(exchange_attend, n, width ** (-0.5) * log2e),
+        out_shape=jax.ShapeDtypeStruct((rows, heads * width), query.dtype),
+        in_specs=[pl.BlockSpec(memory_space=pl.ANY)] * 5 + [pl.BlockSpec(memory_space=pltpu.VMEM)],
+        out_specs=pl.BlockSpec(memory_space=pltpu.VMEM),
+        scratch_shapes=[
+            pltpu.VMEM((n, rows, width), query.dtype),
+            pltpu.VMEM((2 * n, rows, width), query.dtype),
+            pltpu.VMEM((2 * n, rows, width), query.dtype),
+            pltpu.VMEM((n, rows, width), query.dtype),
+            pltpu.SemaphoreType.DMA((5, n)),
+            pltpu.SemaphoreType.DMA((5, n)),
+            pltpu.SemaphoreType.DMA((5,)),
+            pltpu.SemaphoreType.DMA((n,)),
+            pltpu.SemaphoreType.DMA((n,)),
+        ],
+        compiler_params=pltpu.CompilerParams(
+            collective_id=0, has_side_effects=True, vmem_limit_bytes=32 << 20),
+    )(query, key, value, mem_key, mem_value, bias)
+    mixed = jnp.dot(columns, weights, preferred_element_type=jnp.float32)
+    return mixed.astype(query.dtype)[None]
+
+
 def solution(mesh):
     in_specs = (
         P("grp", None, "seq", None),
@@ -94,6 +239,18 @@
         P("seq", None),
     )
     out_specs = P("grp", "seq", None)
-    return jax.shard_map(
-        per_device, mesh=mesh, in_specs=in_specs, out_specs=out_specs, check_vma=False
-    )
+
+    def program(query, key, value, mem_key, mem_value, mem_count, mem_factor, out_weight):
+        direct = (
+            query.shape[0] == mesh.shape["grp"]
+            and query.shape[1] == mesh.shape["seq"]
+            and query.shape[1] % 8 == 0
+            and query.shape[2] == mem_key.shape[2]
+            and (query.shape[2] // mesh.shape["seq"]) % 16 == 0
+        )
+        body = per_device_direct if direct else per_device
+        return jax.shard_map(
+            body, mesh=mesh, in_specs=in_specs, out_specs=out_specs, check_vma=False
+        )(query, key, value, mem_key, mem_value, mem_count, mem_factor, out_weight)
+
+    return program

time: 154 us -> 152 us (0.987)
  blocking collectives: 73.4 us -> 0 us
  Pallas kernels: 0 us -> 72.5 us
  waiting for transfers between devices: 38.3 us -> 52.6 us
  starting transfers between devices: 9.82 us -> 0.01 us
  other arithmetic: 4.96 us -> 0.78 us
  matrix products: 11.3 us -> 7.62 us
  local copies, waits for them, and re-layouts: 1.47 us -> 4.74 us
    all_to_all x4 -> x0, blocking collectives: 73.4 us -> none  [the longest x1 20.1 us: per_device(): lax.all_to_all(attended, 'seq', split_axis=1, concat_axis=0, tiled=True)]
    pallas_call x0 -> x1, Pallas kernels: none -> 72.5 us  [per_device_direct(): pl.pallas_call(functools.partial(exchange_attend, n, width ** (-0.5) * lo...]
    all_gather x1, waiting for transfers between devices: 9.63 us -> 51.9 us  [per_device_direct(): weights = lax.all_gather(out_weight, 'seq', axis=0, tiled=True)]
    all_to_all x2 -> x0, waiting for transfers between devices: 28 us -> none  [the longest x1 14.5 us: per_device(): lax.all_to_all(own_queries, 'seq', split_axis=0, concat_axis=1, tiled=True)]
    all_to_all x2 -> x0, starting transfers between devices: 9.82 us -> none  [the longest x1 5.87 us: per_device(): lax.all_to_all(own_queries, 'seq', split_axis=0, concat_axis=1, tiled=True)]
    unnamed x4 -> x10, local copies, waits for them, and re-layouts: 0.88 us -> 4.74 us
    dot_general x5 -> x1, matrix products: 11.3 us -> 7.62 us  [per_device_direct(): mixed = jnp.dot(columns, weights, preferred_element_type=jnp.float32)]
    unnamed x1 -> x0, other arithmetic: 2.21 us -> none
  transfers between devices with their start and end apart: 3 -> 1, of which waited for: 3 -> 1; matrix products, arithmetic and copies ran while one was open for 7% -> 1% of each run, Pallas kernels for 0% -> 48%
where the time goes in v1:
time: 152 us
  Pallas kernels  72.5 us (48%)
  waiting for transfers between devices  52.6 us (35%)
  between operations  13.4 us (9%)
  matrix products  7.62 us (5%)
  local copies, waits for them, and re-layouts  4.74 us (3%)
    pallas_call x1, Pallas kernels, per_device_direct(): pl.pallas_call(functools.partial(exchange_attend, n, width ** (-0.5) * lo...  72.5 us
    all_gather x1, waiting for transfers between devices, per_device_direct(): weights = lax.all_gather(out_weight, 'seq', axis=0, tiled=True)  51.9 us
    dot_general x1, matrix products, per_device_direct(): mixed = jnp.dot(columns, weights, preferred_element_type=jnp.float32)  7.62 us
    unnamed x10, local copies, waits for them, and re-layouts  4.74 us
  transfers between devices with their start and end apart: 1, of which 1 were waited for; matrix products, arithmetic and copies ran while one was open for 1% of the time, Pallas kernels for 48%

profile of v1, /device:TPU:0, one launch (start us, length us, event | category | flops | bytes accessed | tf_op | source)
XLA Modules:
  0.0 151.7 jit_solution(5211851303158734078)
XLA Ops:
  6.5 0.0 all-gather.2.cloned.1.call-start
  6.5 0.7 all-gather.2.cloned.1.call-update
  7.3 0.8 select_reduce_fusion.1
  8.1 0.0 copy-start
  8.1 0.9 copy-done
  9.0 0.0 copy-start.1
  9.0 0.9 copy-done.1
  10.0 0.0 copy-start.2
  10.0 0.9 copy-done.2
  10.9 0.0 copy-start.3
  10.9 0.9 copy-done.3
  11.9 0.0 copy-start.4
  11.9 0.9 copy-done.4
  12.8 72.5 %shard_map.82 = bf16[64,2048]{1,0:T(8,128)(2,1)S(1)} custom-call(bf16[1,16,64,128]{3,2,1,0:T(8,128)(2,1)S(1)} %copy-done, bf16[1,16,64,128]{3,2,1,0:T(8,128)(2,1)S(1)} %copy-done.1, bf16[1,16,64,128]{3,2,1,0:T(8,128)(2,1)S(1)} %copy-done.2, bf16[1,16,64,128]{3,2,1,0:T(8,128)(2,1)S(1)} %copy-done.3, bf16[1,16,64,128]{3,2,1,0:T(8,128)(2,1)S(1)} %copy-done.4, ...), custom_call_target="tpu_custom_call" | custom-call | tf_op jit(solution)/shard_map/pallas_call | solution.py:207
  85.4 51.9 %all-gather.2.cloned.1.call-done = bf16[2048,3072]{1,0:T(8,128)(2,1)} async-done(((bf16[128,3072]{1,0:T(8,128)(2,1)}), bf16[2048,3072]{1,0:T(8,128)(2,1)}) %all-gather.2.cloned.1.call-update) | async-done | bytes 12582928 | tf_op jit(solution)/shard_map/all_gather | solution.py:206
  137.2 7.6 %fusion = bf16[1,64,3072]{2,1,0:T(8,128)(2,1)} fusion(bf16[64,2048]{1,0:T(8,128)(2,1)S(1)} %shard_map.82, bf16[2048,3072]{1,0:T(8,128)(2,1)} %all-gather.2.cloned.1.call-done), kind=kOutput, calls=%fused_computation.1 | convolution fusion | flops 805502976 | bytes 13238272 | tf_op jit(solution)/shard_map/dot_general | solution.py:226
  (3 shorter events, 0.0 us)
Async XLA Ops:
  6.5 130.7 %all-gather.2.cloned.1.call-start = ((), (), s32[]{:S(2)}) async-start(), calls=%async_computation | async-start | bytes 13369344 | tf_op jit(solution)/shard_map/all_gather | solution.py:206
  8.1 1.0 copy-start
  9.0 0.9 copy-start.1
  10.0 0.9 copy-start.2
  10.9 0.9 copy-start.3
  11.9 0.9 copy-start.4
Sparse Core Ops, SparseCore 0:
  9.6 127.5 all-gather.1

commit v2 on v1

--- a/solution.py
+++ b/solution.py
@@ -87,74 +87,155 @@
     return result
 
 
-def exchange_attend(n, scale2, q_hbm, k_hbm, v_hbm, mk_hbm, mv_hbm, bias_ref, out_ref,
-                    qbuf, kbuf, vbuf, att, in_send, in_recv, own_sem, ret_send, ret_recv):
+def block_kernel(n, nz, scale2, q_hbm, k_hbm, v_hbm, mk_hbm, mv_hbm, w_hbm, bias_ref, out_ref,
+                 qbuf, kbuf, vbuf, att, wbuf, cols, mine, theirs, landed,
+                 in_send, in_recv, own_sem, w_sem, sib_send, sib_recv, up_send, up_recv,
+                 y_send, y_recv, core_send, core_recv, ret_send, ret_recv, out_send, out_recv):
     me = lax.axis_index("seq")
+    g = lax.axis_index("grp")
+    plane = n // nz
+    z, x, c = me // plane, lax.rem(me // 2, 2), lax.rem(me, 2)
     rows, width = qbuf.shape[1], qbuf.shape[2]
+    sibling = me + 1 - 2 * c
+    across = me + 2 - 4 * x
+    mesh_id = pl.DeviceIdType.MESH
 
     barrier = pltpu.get_barrier_semaphore()
 
     @pl.loop(1, n)
     def _(step):
         pl.semaphore_signal(barrier, inc=1, device_id={"seq": lax.rem(me + step, n)},
-                            device_id_type=pl.DeviceIdType.MESH)
-
-    pl.semaphore_wait(barrier, n - 1)
+                            device_id_type=mesh_id)
+
+    pl.semaphore_signal(barrier, inc=1, device_id={"grp": 1 - g}, device_id_type=mesh_id)
+    pl.semaphore_wait(barrier, n)
 
     streams = (
         (q_hbm, qbuf, 0), (k_hbm, kbuf, 0), (mk_hbm, kbuf, n), (v_hbm, vbuf, 0), (mv_hbm, vbuf, n),
     )
 
-    def sending(a, peer):
+    def moving(a, peer, lands):
         src, dst, base = streams[a]
         return pltpu.make_async_remote_copy(
-            src_ref=src.at[0, peer], dst_ref=dst.at[base + me],
-            send_sem=in_send.at[a, peer], recv_sem=in_recv.at[a, me],
-            device_id={"seq": peer}, device_id_type=pl.DeviceIdType.MESH)
-
-    def arriving(a, peer):
-        src, dst, base = streams[a]
-        return pltpu.make_async_remote_copy(
-            src_ref=src.at[0, peer], dst_ref=dst.at[base + peer],
-            send_sem=in_send.at[a, peer], recv_sem=in_recv.at[a, peer],
-            device_id={"seq": peer}, device_id_type=pl.DeviceIdType.MESH)
+            src_ref=src.at[0, peer], dst_ref=dst.at[base + lands],
+            send_sem=in_send.at[a, peer], recv_sem=in_recv.at[a, lands],
+            device_id={"seq": peer}, device_id_type=mesh_id)
 
     def own(a):
         src, dst, base = streams[a]
         return pltpu.make_async_copy(src.at[0, me], dst.at[base + me], own_sem.at[a])
+
+    def wait_inputs(group):
+        for a in group:
+            own(a).wait()
+
+        @pl.loop(1, n)
+        def _(step):
+            peer = lax.rem(me + step, n)
+            for a in group:
+                moving(a, peer, peer).wait_recv()
+
+    def along(d, level, from_own):
+        slot = level * 2 + c
+        return pltpu.make_async_remote_copy(
+            src_ref=w_hbm.at[g] if from_own else wbuf.at[slot, g], dst_ref=wbuf.at[slot, g],
+            send_sem=up_send.at[level], recv_sem=up_recv.at[level],
+            device_id={"seq": lax.rem(me + d * plane + n, n)}, device_id_type=mesh_id)
+
+    def along_own(i, d):
+        return pltpu.make_async_remote_copy(
+            src_ref=w_hbm.at[g], dst_ref=wbuf.at[z * 2 + c, g],
+            send_sem=up_send.at[nz + i], recv_sem=up_recv.at[z],
+            device_id={"seq": lax.rem(me + d * plane + n, n)}, device_id_type=mesh_id)
+
+    def over_y(level, half):
+        slot = level * 2 + c
+        return pltpu.make_async_remote_copy(
+            src_ref=wbuf.at[slot, half], dst_ref=wbuf.at[slot, half],
+            send_sem=y_send.at[level], recv_sem=y_recv.at[level],
+            device_id={"grp": 1 - g}, device_id_type=mesh_id)
+
+    def over_core(level, half, core):
+        slot = level * 2 + core
+        return pltpu.make_async_remote_copy(
+            src_ref=wbuf.at[slot, half], dst_ref=wbuf.at[slot, half],
+            send_sem=core_send.at[level, half], recv_sem=core_recv.at[level, half],
+            device_id={"seq": sibling}, device_id_type=mesh_id)
+
+    def to_sibling(core):
+        return pltpu.make_async_remote_copy(
+            src_ref=w_hbm, dst_ref=wbuf.at[z * 2 + core], send_sem=sib_send, recv_sem=sib_recv,
+            device_id={"seq": sibling}, device_id_type=mesh_id)
+
+    def each_level(s, act):
+        for d in (1, -1):
+            level = z - d * s
+
+            @pl.when((level >= 0) & (level < nz))
+            def _():
+                act(d, level)
+
+    def each_forward(s, act):
+        for d in (1, -1):
+            level = z - d * s
+
+            @pl.when((level >= 0) & (level < nz) & (z + d >= 0) & (z + d < nz))
+            def _():
+                act(d, level)
+
+    def take_chain(s):
+        each_level(s, lambda d, level: along(d, level, False).wait_recv())
+        if s < nz - 1:
+            each_forward(s, lambda d, level: along(d, level, False).start())
+        each_level(s, lambda d, level: over_y(level, g).start())
+        each_level(s, lambda d, level: over_core(level, g, c).start())
+
+    def take_y(s):
+        def act(d, level):
+            over_y(level, 1 - g).wait_recv()
+            over_core(level, 1 - g, c).start()
+        each_level(s, act)
 
     for group in ((0, 1, 2), (3, 4)):
         @pl.loop(0, n - 1)
         def _(k):
             peer = lax.rem(me + 1 + lax.rem(k + n // 2 - 1, n - 1), n)
             for a in group:
-                sending(a, peer).start()
+                moving(a, peer, me).start()
+    for i, d in enumerate((1, -1)):
+        @pl.when((z + d >= 0) & (z + d < nz))
+        def _():
+            along_own(i, d).start()
+    to_sibling(c).start()
     for a in range(5):
         own(a).start()
-    for a in range(5):
-        own(a).wait()
-
-    @pl.loop(1, n)
-    def _(step):
-        peer = lax.rem(me + step, n)
-        for a in range(5):
-            arriving(a, peer).wait_recv()
+    own_weight = pltpu.make_async_copy(w_hbm, wbuf.at[z * 2 + c], w_sem)
+    own_weight.start()
+
+    take_chain(1)
+    wait_inputs((0, 1, 2))
+    take_chain(2)
+    take_y(1)
+    wait_inputs((3, 4))
 
     keys = kbuf[...].reshape(2 * n * rows, width)
     vals = vbuf[...].reshape(2 * n * rows, width)
-    parts = n // 4
-
-    def returning(owner):
-        return pltpu.make_async_remote_copy(
-            src_ref=att.at[owner],
-            dst_ref=out_ref.at[:, pl.ds(pl.multiple_of(me * width, width), width)],
-            send_sem=ret_send.at[owner], recv_sem=ret_recv.at[me],
-            device_id={"seq": owner}, device_id_type=pl.DeviceIdType.MESH)
-
-    @pl.loop(0, parts)
+    head = z * 2 + c
+
+    def lanes(h):
+        return pl.ds(pl.multiple_of(h * width, width), width)
+
+    def returning(level, xr, core):
+        owner = level * plane + xr * 2 + core
+        return pltpu.make_async_remote_copy(
+            src_ref=att.at[owner], dst_ref=cols.at[lax.rem(xr + x, 2), :, lanes(head)],
+            send_sem=ret_send.at[owner], recv_sem=ret_recv.at[lax.rem(xr + x, 2), head],
+            device_id={"seq": level * plane + x * 2 + core}, device_id_type=mesh_id)
+
+    @pl.loop(0, nz)
     def _(j):
-        block = lax.rem(me // 4 + parts // 2 + j, parts)
-        queries = qbuf[pl.ds(block * 4, 4)].reshape(4 * rows, width)
+        level = lax.rem(z + nz // 2 + j, nz)
+        queries = qbuf[pl.ds(level * plane, plane)].reshape(plane * rows, width)
         score = lax.dot_general(queries, keys, (((1,), (1,)), ((), ())),
                                 preferred_element_type=jnp.float32)
         score = score * scale2 + bias_ref[...]
@@ -162,30 +243,91 @@
         prob = jnp.exp2(score - top)
         total = jnp.sum(prob, axis=1, keepdims=True)
         mixed = jnp.dot(prob.astype(jnp.bfloat16), vals, preferred_element_type=jnp.float32)
-        att[pl.ds(block * 4, 4)] = (mixed / total).astype(jnp.bfloat16).reshape(4, rows, width)
-        for t in range(4):
-            owner = block * 4 + t
-
-            @pl.when(owner != me)
+        att[pl.ds(level * plane, plane)] = (
+            (mixed / total).astype(jnp.bfloat16).reshape(plane, rows, width))
+        for core in range(2):
+            for xr in range(2):
+                @pl.when((level != z) | (core != c))
+                def _():
+                    returning(level, xr, core).start()
+
+    for xr in range(2):
+        keep = pltpu.make_async_copy(
+            att.at[z * plane + xr * 2 + c], cols.at[lax.rem(xr + x, 2), :, lanes(head)],
+            own_sem.at[xr])
+        keep.start()
+        keep.wait()
+
+    take_chain(3)
+    take_y(2)
+    take_y(3)
+    own_weight.wait()
+    to_sibling(1 - c).wait_recv()
+
+    def last_core(d, level):
+        for half in range(2):
+            over_core(level, half, 1 - c).wait_recv()
+
+    for s in range(1, nz):
+        each_level(s, last_core)
+
+    @pl.loop(0, 2 * nz)
+    def _(h):
+        for slot in range(2):
+            @pl.when(h != head)
             def _():
-                returning(owner).start()
-
-    mine = pltpu.make_async_copy(
-        att.at[me], out_ref.at[:, pl.ds(pl.multiple_of(me * width, width), width)], own_sem.at[0])
-    mine.start()
-    mine.wait()
+                pltpu.make_async_remote_copy(
+                    src_ref=att.at[0], dst_ref=cols.at[slot, :, lanes(h)],
+                    send_sem=ret_send.at[0], recv_sem=ret_recv.at[slot, h],
+                    device_id={"seq": sibling}, device_id_type=mesh_id).wait_recv()
+
+    tiles, tile = landed.shape[0], landed.shape[2]
+    left = jnp.concatenate([cols[0], cols[1]], 0)
+
+    def crossing(t):
+        return pltpu.make_async_remote_copy(
+            src_ref=theirs.at[t], dst_ref=landed.at[t],
+            send_sem=out_send.at[t], recv_sem=out_recv.at[t],
+            device_id={"seq": across}, device_id_type=mesh_id)
+
+    for t in range(tiles):
+        right = wbuf[:, :, :, t * tile:(t + 1) * tile].reshape(2 * nz * width, tile)
+        mixed = jnp.dot(left, right, preferred_element_type=jnp.float32)
+        theirs[t] = mixed[rows:].astype(jnp.bfloat16)
+        crossing(t).start()
+        mine[t] = mixed[:rows]
+    for t in range(tiles):
+        crossing(t).wait_recv()
+        out_ref[:, t * tile:(t + 1) * tile] = (
+            mine[t] + landed[t].astype(jnp.float32)).astype(out_ref.dtype)
 
     @pl.loop(1, n)
     def _(step):
         peer = lax.rem(me + step, n)
         for a in range(5):
-            sending(a, peer).wait_send()
-        returning(peer).wait_send()
-        pltpu.make_async_remote_copy(
-            src_ref=att.at[peer],
-            dst_ref=out_ref.at[:, pl.ds(pl.multiple_of(peer * width, width), width)],
-            send_sem=ret_send.at[peer], recv_sem=ret_recv.at[peer],
-            device_id={"seq": peer}, device_id_type=pl.DeviceIdType.MESH).wait_recv()
+            moving(a, peer, me).wait_send()
+
+    @pl.loop(0, nz)
+    def _(level):
+        for core in range(2):
+            for xr in range(2):
+                @pl.when((level != z) | (core != c))
+                def _():
+                    returning(level, xr, core).wait_send()
+
+    for i, d in enumerate((1, -1)):
+        @pl.when((z + d >= 0) & (z + d < nz))
+        def _():
+            along_own(i, d).wait_send()
+    for s in range(1, nz - 1):
+        each_forward(s, lambda d, level: along(d, level, False).wait_send())
+    for s in range(1, nz):
+        each_level(s, lambda d, level: over_y(level, g).wait_send())
+        each_level(s, lambda d, level: over_core(level, 0, c).wait_send())
+        each_level(s, lambda d, level: over_core(level, 1, c).wait_send())
+    to_sibling(c).wait_send()
+    for t in range(tiles):
+        crossing(t).wait_send()
 
 
 def full_bias_of(counts, factors, length, slots):
@@ -203,28 +345,34 @@
     n = heads
     log2e = math.log2(math.e)
     bias = full_bias_of(mem_count[0], mem_factor[0], n * rows, n * rows) * log2e
-    weights = lax.all_gather(out_weight, "seq", axis=0, tiled=True)
-    columns = pl.pallas_call(
-        functools.partial(exchange_attend, n, width ** (-0.5) * log2e),
-        out_shape=jax.ShapeDtypeStruct((rows, heads * width), query.dtype),
-        in_specs=[pl.BlockSpec(memory_space=pl.ANY)] * 5 + [pl.BlockSpec(memory_space=pltpu.VMEM)],
+    depth, feat = out_weight.shape
+    nz = n // 4
+    tile = 512
+    bf16 = query.dtype
+    dma = pltpu.SemaphoreType.DMA
+    result = pl.pallas_call(
+        functools.partial(block_kernel, n, nz, width ** (-0.5) * log2e),
+        out_shape=jax.ShapeDtypeStruct((rows, feat), bf16),
+        in_specs=[pl.BlockSpec(memory_space=pltpu.HBM)] * 6 + [pl.BlockSpec(memory_space=pltpu.VMEM)],
         out_specs=pl.BlockSpec(memory_space=pltpu.VMEM),
         scratch_shapes=[
-            pltpu.VMEM((n, rows, width), query.dtype),
-            pltpu.VMEM((2 * n, rows, width), query.dtype),
-            pltpu.VMEM((2 * n, rows, width), query.dtype),
-            pltpu.VMEM((n, rows, width), query.dtype),
-            pltpu.SemaphoreType.DMA((5, n)),
-            pltpu.SemaphoreType.DMA((5, n)),
-            pltpu.SemaphoreType.DMA((5,)),
-            pltpu.SemaphoreType.DMA((n,)),
-            pltpu.SemaphoreType.DMA((n,)),
+            pltpu.VMEM((n, rows, width), bf16),
+            pltpu.VMEM((2 * n, rows, width), bf16),
+            pltpu.VMEM((2 * n, rows, width), bf16),
+            pltpu.VMEM((n, rows, width), bf16),
+            pltpu.VMEM((2 * nz, 2, depth // 2, feat), bf16),
+            pltpu.VMEM((2, rows, 2 * nz * width), bf16),
+            pltpu.VMEM((feat // tile, rows, tile), jnp.float32),
+            pltpu.VMEM((feat // tile, rows, tile), bf16),
+            pltpu.VMEM((feat // tile, rows, tile), bf16),
+            dma((5, n)), dma((5, n)), dma((5,)), dma, dma, dma, dma((nz + 2,)), dma((nz,)),
+            dma((nz,)), dma((nz,)), dma((nz, 2)), dma((nz, 2)), dma((n,)), dma((2, 2 * nz)),
+            dma((feat // tile,)), dma((feat // tile,)),
         ],
         compiler_params=pltpu.CompilerParams(
-            collective_id=0, has_side_effects=True, vmem_limit_bytes=32 << 20),
-    )(query, key, value, mem_key, mem_value, bias)
-    mixed = jnp.dot(columns, weights, preferred_element_type=jnp.float32)
-    return mixed.astype(query.dtype)[None]
+            collective_id=0, has_side_effects=True, vmem_limit_bytes=62 << 20),
+    )(query, key, value, mem_key, mem_value, out_weight.reshape(2, depth // 2, feat), bias)
+    return result[None]
 
 
 def solution(mesh):
@@ -244,7 +392,11 @@
         direct = (
             query.shape[0] == mesh.shape["grp"]
             and query.shape[1] == mesh.shape["seq"]
-            and query.shape[1] % 8 == 0
+            and mesh.shape["grp"] == 2
+            and query.shape[1] == 16
+            and out_weight.shape[0] == query.shape[1] * query.shape[3]
+            and query.shape[3] == 128
+            and out_weight.shape[1] % 512 == 0
             and query.shape[2] == mem_key.shape[2]
             and (query.shape[2] // mesh.shape["seq"]) % 16 == 0
         )

time: 152 us -> 91.8 us (0.60)
  waiting for transfers between devices: 52.6 us -> 0 us
  Pallas kernels: 72.5 us -> 88.1 us
  between operations: 13.4 us -> 0.02 us
  matrix products: 7.62 us -> 0 us
  local copies, waits for them, and re-layouts: 4.74 us -> 2.43 us
    all_gather x1 -> x0, waiting for transfers between devices: 51.9 us -> none  [per_device_direct(): weights = lax.all_gather(out_weight, 'seq', axis=0, tiled=True)]
    pallas_call x1, Pallas kernels: 72.5 us -> 88.1 us  [per_device_direct(): pl.pallas_call(functools.partial(block_kernel, n, nz, width ** (-0.5) * l...]
    dot_general x1 -> x0, matrix products: 7.62 us -> none  [per_device_direct(): mixed = jnp.dot(columns, weights, preferred_element_type=jnp.float32)]
    unnamed x10 -> x5, local copies, waits for them, and re-layouts: 4.74 us -> 2.43 us
  transfers between devices with their start and end apart: 1 -> 0, of which waited for: 1 -> 0; matrix products, arithmetic and copies ran while one was open for 1% -> 0% of each run, Pallas kernels for 48% -> 0%
where the time goes in v2:
time: 91.8 us; the launch traced here: 91.3 us
  Pallas kernels  88.1 us (96%)
  local copies, waits for them, and re-layouts  2.43 us (3%)
    pallas_call x1, Pallas kernels, per_device_direct(): pl.pallas_call(functools.partial(block_kernel, n, nz, width ** (-0.5) * l...  88.1 us
    unnamed x5, local copies, waits for them, and re-layouts  2.43 us

profile of v2, /device:TPU:0, one launch (start us, length us, event | category | flops | bytes accessed | tf_op | source)
XLA Modules:
  0.0 91.3 jit_solution(17610029837139270923)
XLA Ops:
  0.0 0.0 copy-start
  0.0 0.0 copy-start.1
  0.0 0.6 copy-done
  0.7 0.0 copy-done.1
  0.7 0.1 select_reduce_fusion.1
  0.8 0.6 pad_multiply_fusion
  1.4 88.1 %shard_map.82 = bf16[64,3072]{1,0:T(8,128)(2,1)} custom-call(bf16[1,16,64,128]{3,2,1,0:T(8,128)(2,1)} %q_hbm.1, bf16[1,16,64,128]{3,2,1,0:T(8,128)(2,1)} %k_hbm.1, bf16[1,16,64,128]{3,2,1,0:T(8,128)(2,1)} %v_hbm.1, bf16[1,16,64,128]{3,2,1,0:T(8,128)(2,1)} %mk_hbm.1, bf16[1,16,64,128]{3,2,1,0:T(8,128)(2,1)} %mv_hbm.1, bf16[2,64,3072]{2,1,0:T(8,128)(2,1)} %bitcast.6, ...), custom_call_target="tpu_custom_call" | custom-call | tf_op jit(solution)/shard_map/pallas_call | solution.py:353
  89.5 1.8 %copy.10 = bf16[1,64,3072]{2,1,0:T(8,128)(2,1)} copy(bf16[1,64,3072]{2,1,0:T(8,128)(2,1)} %bitcast.5) | data formatting | bytes 786432
  (2 shorter events, 0.0 us)
Async XLA Ops:
  0.0 0.7 copy-start
  0.0 0.7 copy-start.1

commit v3 on v2

--- a/solution.py
+++ b/solution.py
@@ -87,8 +87,12 @@
     return result
 
 
-def block_kernel(n, nz, scale2, q_hbm, k_hbm, v_hbm, mk_hbm, mv_hbm, w_hbm, bias_ref, out_ref,
-                 qbuf, kbuf, vbuf, att, wbuf, cols, mine, theirs, landed,
+LOG2E = math.log2(math.e)
+PIECES = 2
+
+
+def block_kernel(n, nz, scale2, q_hbm, k_hbm, v_hbm, mk_hbm, mv_hbm, w_hbm, count_ref, factor_ref, out_ref,
+                 qbuf, kbuf, vbuf, att, wbuf, cols, mine, theirs, landed, bias_ref,
                  in_send, in_recv, own_sem, w_sem, sib_send, sib_recv, up_send, up_recv,
                  y_send, y_recv, core_send, core_recv, ret_send, ret_recv, out_send, out_recv):
     me = lax.axis_index("seq")
@@ -135,37 +139,47 @@
             for a in group:
                 moving(a, peer, peer).wait_recv()
 
-    def along(d, level, from_own):
+    pieces, span = wbuf.shape[0], wbuf.shape[4]
+
+    def columns(p):
+        return pl.ds(p * span, span)
+
+    def along(d, level, p):
         slot = level * 2 + c
         return pltpu.make_async_remote_copy(
-            src_ref=w_hbm.at[g] if from_own else wbuf.at[slot, g], dst_ref=wbuf.at[slot, g],
-            send_sem=up_send.at[level], recv_sem=up_recv.at[level],
+            src_ref=wbuf.at[p, slot, g], dst_ref=wbuf.at[p, slot, g],
+            send_sem=up_send.at[level, p], recv_sem=up_recv.at[level, p],
             device_id={"seq": lax.rem(me + d * plane + n, n)}, device_id_type=mesh_id)
 
-    def along_own(i, d):
-        return pltpu.make_async_remote_copy(
-            src_ref=w_hbm.at[g], dst_ref=wbuf.at[z * 2 + c, g],
-            send_sem=up_send.at[nz + i], recv_sem=up_recv.at[z],
+    def along_own(i, d, p):
+        return pltpu.make_async_remote_copy(
+            src_ref=w_hbm.at[g, :, columns(p)], dst_ref=wbuf.at[p, z * 2 + c, g],
+            send_sem=up_send.at[nz + i, p], recv_sem=up_recv.at[z, p],
             device_id={"seq": lax.rem(me + d * plane + n, n)}, device_id_type=mesh_id)
 
-    def over_y(level, half):
+    def over_y(level, half, p):
         slot = level * 2 + c
         return pltpu.make_async_remote_copy(
-            src_ref=wbuf.at[slot, half], dst_ref=wbuf.at[slot, half],
-            send_sem=y_send.at[level], recv_sem=y_recv.at[level],
+            src_ref=wbuf.at[p, slot, half], dst_ref=wbuf.at[p, slot, half],
+            send_sem=y_send.at[level, p], recv_sem=y_recv.at[level, p],
             device_id={"grp": 1 - g}, device_id_type=mesh_id)
 
-    def over_core(level, half, core):
+    def over_core(level, half, core, p):
         slot = level * 2 + core
         return pltpu.make_async_remote_copy(
-            src_ref=wbuf.at[slot, half], dst_ref=wbuf.at[slot, half],
-            send_sem=core_send.at[level, half], recv_sem=core_recv.at[level, half],
+            src_ref=wbuf.at[p, slot, half], dst_ref=wbuf.at[p, slot, half],
+            send_sem=core_send.at[level, half, p], recv_sem=core_recv.at[level, half, p],
             device_id={"seq": sibling}, device_id_type=mesh_id)
 
-    def to_sibling(core):
-        return pltpu.make_async_remote_copy(
-            src_ref=w_hbm, dst_ref=wbuf.at[z * 2 + core], send_sem=sib_send, recv_sem=sib_recv,
+    def to_sibling(core, p):
+        return pltpu.make_async_remote_copy(
+            src_ref=w_hbm.at[:, :, columns(p)], dst_ref=wbuf.at[p, z * 2 + core],
+            send_sem=sib_send.at[p], recv_sem=sib_recv.at[p],
             device_id={"seq": sibling}, device_id_type=mesh_id)
+
+    def own_weight(p):
+        return pltpu.make_async_copy(
+            w_hbm.at[:, :, columns(p)], wbuf.at[p, z * 2 + c], w_sem.at[p])
 
     def each_level(s, act):
         for d in (1, -1):
@@ -183,17 +197,17 @@
             def _():
                 act(d, level)
 
-    def take_chain(s):
-        each_level(s, lambda d, level: along(d, level, False).wait_recv())
+    def take_chain(s, p):
+        each_level(s, lambda d, level: along(d, level, p).wait_recv())
         if s < nz - 1:
-            each_forward(s, lambda d, level: along(d, level, False).start())
-        each_level(s, lambda d, level: over_y(level, g).start())
-        each_level(s, lambda d, level: over_core(level, g, c).start())
-
-    def take_y(s):
+            each_forward(s, lambda d, level: along(d, level, p).start())
+        each_level(s, lambda d, level: over_y(level, g, p).start())
+        each_level(s, lambda d, level: over_core(level, g, c, p).start())
+
+    def take_y(s, p):
         def act(d, level):
-            over_y(level, 1 - g).wait_recv()
-            over_core(level, 1 - g, c).start()
+            over_y(level, 1 - g, p).wait_recv()
+            over_core(level, 1 - g, c, p).start()
         each_level(s, act)
 
     for group in ((0, 1, 2), (3, 4)):
@@ -205,18 +219,29 @@
     for i, d in enumerate((1, -1)):
         @pl.when((z + d >= 0) & (z + d < nz))
         def _():
-            along_own(i, d).start()
-    to_sibling(c).start()
+            for p in range(pieces):
+                along_own(i, d, p).start()
+    for p in range(pieces):
+        to_sibling(c, p).start()
     for a in range(5):
         own(a).start()
-    own_weight = pltpu.make_async_copy(w_hbm, wbuf.at[z * 2 + c], w_sem)
-    own_weight.start()
-
-    take_chain(1)
-    wait_inputs((0, 1, 2))
-    take_chain(2)
-    take_y(1)
-    wait_inputs((3, 4))
+    for p in range(pieces):
+        own_weight(p).start()
+
+    for s in (1, 2):
+        for p in range(pieces):
+            take_chain(s, p)
+    for p in range(pieces):
+        take_y(1, p)
+    wait_inputs((0, 1, 2, 3, 4))
+
+    slot_at = lax.broadcasted_iota(jnp.int32, (1, MCAP), 1)
+    parts = [jnp.zeros((1, n * rows), jnp.float32)]
+    for s in range(count_ref.shape[1]):
+        factor = jnp.full((1, MCAP), factor_ref[0, s], jnp.int32).astype(jnp.float32)
+        parts.append(jnp.where(slot_at < count_ref[0, s], jnp.log(factor) * LOG2E,
+                               jnp.float32(-1.0e9)))
+    bias_ref[...] = jnp.concatenate(parts, 1)
 
     keys = kbuf[...].reshape(2 * n * rows, width)
     vals = vbuf[...].reshape(2 * n * rows, width)
@@ -232,8 +257,7 @@
             send_sem=ret_send.at[owner], recv_sem=ret_recv.at[lax.rem(xr + x, 2), head],
             device_id={"seq": level * plane + x * 2 + core}, device_id_type=mesh_id)
 
-    @pl.loop(0, nz)
-    def _(j):
+    def attend(j):
         level = lax.rem(z + nz // 2 + j, nz)
         queries = qbuf[pl.ds(level * plane, plane)].reshape(plane * rows, width)
         score = lax.dot_general(queries, keys, (((1,), (1,)), ((), ())),
@@ -251,6 +275,15 @@
                 def _():
                     returning(level, xr, core).start()
 
+    for j in range(nz):
+        attend(j)
+        if j == 1:
+            take_chain(3, 0)
+            take_y(2, 0)
+        if j == 2:
+            for p in range(1, pieces):
+                take_chain(3, p)
+
     for xr in range(2):
         keep = pltpu.make_async_copy(
             att.at[z * plane + xr * 2 + c], cols.at[lax.rem(xr + x, 2), :, lanes(head)],
@@ -258,18 +291,18 @@
         keep.start()
         keep.wait()
 
-    take_chain(3)
-    take_y(2)
-    take_y(3)
-    own_weight.wait()
-    to_sibling(1 - c).wait_recv()
-
-    def last_core(d, level):
-        for half in range(2):
-            over_core(level, half, 1 - c).wait_recv()
-
-    for s in range(1, nz):
-        each_level(s, last_core)
+    take_y(3, 0)
+    for p in range(1, pieces):
+        take_y(2, p)
+
+    def last_core(p):
+        def act(d, level):
+            for half in range(2):
+                over_core(level, half, 1 - c, p).wait_recv()
+        for s in range(1, nz):
+            each_level(s, act)
+        own_weight(p).wait()
+        to_sibling(1 - c, p).wait_recv()
 
     @pl.loop(0, 2 * nz)
     def _(h):
@@ -291,7 +324,12 @@
             device_id={"seq": across}, device_id_type=mesh_id)
 
     for t in range(tiles):
-        right = wbuf[:, :, :, t * tile:(t + 1) * tile].reshape(2 * nz * width, tile)
+        p, first = t * tile // span, t * tile % span
+        if first == 0:
+            if p:
+                take_y(3, p)
+            last_core(p)
+        right = wbuf[p, :, :, :, first:first + tile].reshape(2 * nz * width, tile)
         mixed = jnp.dot(left, right, preferred_element_type=jnp.float32)
         theirs[t] = mixed[rows:].astype(jnp.bfloat16)
         crossing(t).start()
@@ -318,60 +356,62 @@
     for i, d in enumerate((1, -1)):
         @pl.when((z + d >= 0) & (z + d < nz))
         def _():
-            along_own(i, d).wait_send()
+            for p in range(pieces):
+                along_own(i, d, p).wait_send()
+
+    def sent_on(d, level):
+        for p in range(pieces):
+            over_y(level, g, p).wait_send()
+            over_core(level, 0, c, p).wait_send()
+            over_core(level, 1, c, p).wait_send()
+
+    def forwarded(d, level):
+        for p in range(pieces):
+            along(d, level, p).wait_send()
+
     for s in range(1, nz - 1):
-        each_forward(s, lambda d, level: along(d, level, False).wait_send())
+        each_forward(s, forwarded)
     for s in range(1, nz):
-        each_level(s, lambda d, level: over_y(level, g).wait_send())
-        each_level(s, lambda d, level: over_core(level, 0, c).wait_send())
-        each_level(s, lambda d, level: over_core(level, 1, c).wait_send())
-    to_sibling(c).wait_send()
+        each_level(s, sent_on)
+    for p in range(pieces):
+        to_sibling(c, p).wait_send()
     for t in range(tiles):
         crossing(t).wait_send()
-
-
-def full_bias_of(counts, factors, length, slots):
-    slot = jnp.arange(slots)
-    picked = (slot // MCAP)[:, None] == jnp.arange(counts.shape[0])[None, :]
-    slot_count = jnp.sum(jnp.where(picked, counts[None, :], 0), 1)
-    slot_factor = jnp.sum(jnp.where(picked, factors[None, :], 0), 1)
-    bias = jnp.where(slot % MCAP < slot_count, jnp.log(slot_factor.astype(jnp.float32)),
-                     jnp.float32(-1000000000.0))
-    return jnp.concatenate([jnp.zeros((length,), jnp.float32), bias])[None, :]
 
 
 def per_device_direct(query, key, value, mem_key, mem_value, mem_count, mem_factor, out_weight):
     _, heads, rows, width = query.shape
     n = heads
-    log2e = math.log2(math.e)
-    bias = full_bias_of(mem_count[0], mem_factor[0], n * rows, n * rows) * log2e
     depth, feat = out_weight.shape
     nz = n // 4
     tile = 512
     bf16 = query.dtype
     dma = pltpu.SemaphoreType.DMA
     result = pl.pallas_call(
-        functools.partial(block_kernel, n, nz, width ** (-0.5) * log2e),
+        functools.partial(block_kernel, n, nz, width ** (-0.5) * LOG2E),
         out_shape=jax.ShapeDtypeStruct((rows, feat), bf16),
-        in_specs=[pl.BlockSpec(memory_space=pltpu.HBM)] * 6 + [pl.BlockSpec(memory_space=pltpu.VMEM)],
+        in_specs=[pl.BlockSpec(memory_space=pltpu.HBM)] * 6 + [pl.BlockSpec(memory_space=pltpu.SMEM)] * 2,
         out_specs=pl.BlockSpec(memory_space=pltpu.VMEM),
         scratch_shapes=[
             pltpu.VMEM((n, rows, width), bf16),
             pltpu.VMEM((2 * n, rows, width), bf16),
             pltpu.VMEM((2 * n, rows, width), bf16),
             pltpu.VMEM((n, rows, width), bf16),
-            pltpu.VMEM((2 * nz, 2, depth // 2, feat), bf16),
+            pltpu.VMEM((PIECES, 2 * nz, 2, depth // 2, feat // PIECES), bf16),
             pltpu.VMEM((2, rows, 2 * nz * width), bf16),
             pltpu.VMEM((feat // tile, rows, tile), jnp.float32),
             pltpu.VMEM((feat // tile, rows, tile), bf16),
             pltpu.VMEM((feat // tile, rows, tile), bf16),
-            dma((5, n)), dma((5, n)), dma((5,)), dma, dma, dma, dma((nz + 2,)), dma((nz,)),
-            dma((nz,)), dma((nz,)), dma((nz, 2)), dma((nz, 2)), dma((n,)), dma((2, 2 * nz)),
+            pltpu.VMEM((1, 2 * n * rows), jnp.float32),
+            dma((5, n)), dma((5, n)), dma((5,)), dma((PIECES,)), dma((PIECES,)), dma((PIECES,)),
+            dma((nz + 2, PIECES)), dma((nz, PIECES)), dma((nz, PIECES)), dma((nz, PIECES)),
+            dma((nz, 2, PIECES)), dma((nz, 2, PIECES)), dma((n,)), dma((2, 2 * nz)),
             dma((feat // tile,)), dma((feat // tile,)),
         ],
         compiler_params=pltpu.CompilerParams(
             collective_id=0, has_side_effects=True, vmem_limit_bytes=62 << 20),
-    )(query, key, value, mem_key, mem_value, out_weight.reshape(2, depth // 2, feat), bias)
+    )(query, key, value, mem_key, mem_value, out_weight.reshape(2, depth // 2, feat),
+      mem_count, mem_factor)
     return result[None]
 
 
@@ -396,7 +436,8 @@
             and query.shape[1] == 16
             and out_weight.shape[0] == query.shape[1] * query.shape[3]
             and query.shape[3] == 128
-            and out_weight.shape[1] % 512 == 0
+            and out_weight.shape[1] % (512 * PIECES) == 0
+            and mem_key.shape[2] == mem_count.shape[1] * MCAP
             and query.shape[2] == mem_key.shape[2]
             and (query.shape[2] // mesh.shape["seq"]) % 16 == 0
         )

time: 91.8 us -> 83.5 us (0.910)
  Pallas kernels: 88.1 us -> 81 us
    pallas_call x1, Pallas kernels: 88.1 us -> 81 us  [per_device_direct(): pl.pallas_call(functools.partial(block_kernel, n, nz, width ** (-0.5) * L...]
    unnamed x5 -> x1, local copies, waits for them, and re-layouts: 2.43 us -> 1.77 us
where the time goes in v3:
time: 83.5 us; the launch traced here: 82.8 us
  Pallas kernels  81 us (97%)
  local copies, waits for them, and re-layouts  1.77 us (2%)
    pallas_call x1, Pallas kernels, per_device_direct(): pl.pallas_call(functools.partial(block_kernel, n, nz, width ** (-0.5) * L...  81 us
    unnamed x1, local copies, waits for them, and re-layouts  1.77 us

profile of v3, /device:TPU:0, one launch (start us, length us, event | category | flops | bytes accessed | tf_op | source)
XLA Modules:
  0.0 82.8 jit_solution(14840960240264069443)
XLA Ops:
  0.0 81.0 %shard_map.82 = bf16[64,3072]{1,0:T(8,128)(2,1)} custom-call(bf16[1,16,64,128]{3,2,1,0:T(8,128)(2,1)} %q_hbm.1, bf16[1,16,64,128]{3,2,1,0:T(8,128)(2,1)} %k_hbm.1, bf16[1,16,64,128]{3,2,1,0:T(8,128)(2,1)} %v_hbm.1, bf16[1,16,64,128]{3,2,1,0:T(8,128)(2,1)} %mk_hbm.1, bf16[1,16,64,128]{3,2,1,0:T(8,128)(2,1)} %mv_hbm.1, bf16[2,64,3072]{2,1,0:T(8,128)(2,1)} %bitcast.3, ...), custom_call_target="tpu_custom_call" | custom-call | tf_op jit(solution)/shard_map/pallas_call | solution.py:390
  81.0 1.8 %copy.10 = bf16[1,64,3072]{2,1,0:T(8,128)(2,1)} copy(bf16[1,64,3072]{2,1,0:T(8,128)(2,1)} %bitcast.2) | data formatting | bytes 786432

commit v4 on v3

--- a/solution.py
+++ b/solution.py
@@ -88,7 +88,7 @@
 
 
 LOG2E = math.log2(math.e)
-PIECES = 2
+PIECES = 3
 
 
 def block_kernel(n, nz, scale2, q_hbm, k_hbm, v_hbm, mk_hbm, mv_hbm, w_hbm, count_ref, factor_ref, out_ref,

time: 83.5 us -> 82.4 us (0.987)
  no operation moved by 1% of the time
where the time goes in v4:
time: 82.4 us; the launch traced here: 82.2 us
  Pallas kernels  80.5 us (98%)
  local copies, waits for them, and re-layouts  1.77 us (2%)
    pallas_call x1, Pallas kernels, per_device_direct(): pl.pallas_call(functools.partial(block_kernel, n, nz, width ** (-0.5) * L...  80.5 us
    unnamed x1, local copies, waits for them, and re-layouts  1.77 us

profile of v4, /device:TPU:0, one launch (start us, length us, event | category | flops | bytes accessed | tf_op | source)
XLA Modules:
  0.0 82.2 jit_solution(17220550476956775766)
XLA Ops:
  0.0 80.5 %shard_map.82 = bf16[64,3072]{1,0:T(8,128)(2,1)} custom-call(bf16[1,16,64,128]{3,2,1,0:T(8,128)(2,1)} %q_hbm.1, bf16[1,16,64,128]{3,2,1,0:T(8,128)(2,1)} %k_hbm.1, bf16[1,16,64,128]{3,2,1,0:T(8,128)(2,1)} %v_hbm.1, bf16[1,16,64,128]{3,2,1,0:T(8,128)(2,1)} %mk_hbm.1, bf16[1,16,64,128]{3,2,1,0:T(8,128)(2,1)} %mv_hbm.1, bf16[2,64,3072]{2,1,0:T(8,128)(2,1)} %bitcast.3, ...), custom_call_target="tpu_custom_call" | custom-call | tf_op jit(solution)/shard_map/pallas_call | solution.py:390
  80.5 1.8 %copy.10 = bf16[1,64,3072]{2,1,0:T(8,128)(2,1)} copy(bf16[1,64,3072]{2,1,0:T(8,128)(2,1)} %bitcast.2) | data formatting | bytes 786432
